TPU v7x, 512 devices: a whole 4x8x8 slice. The times are simulated.
512 devices in a mesh: row: 32 (over z_lo, y), col: 16 (over x, z_hi, core).
Axes of the slice: x: 4, y: 8, z: 8 (z_hi: 2, z_lo: 4; z = z_hi * 4 + z_lo), core: 2. Of those that a mesh axis runs over, the one named last changes fastest.
Arguments:
- features: bfloat16 [16, 4096, 128], P('col', 'row'), may hold values from -6 to 6
- weight: bfloat16 [128, 256], replicated, may hold values from -0.5 to 0.5
- tile_values: bfloat16 [32, 16, 32, 128, 128], P('row', 'col'), may hold values from -0.125 to 0.125
- tile_rows: int32 [32, 16, 32], P('row', 'col'), may hold values from 0 to 15
- tile_cols: int32 [32, 16, 32], P('row', 'col'), may hold values from 0 to 31
- tile_count: int32 [32, 16], P('row', 'col'), may hold values from 4 to 32, as said below
- cotangent: bfloat16 [32, 2048, 256], P('row', 'col'), may hold values from -6 to 6
Outputs:
- output: bfloat16 [32, 2048, 256], P('row', 'col')
- grad_features: bfloat16 [16, 4096, 128], P('col', 'row')
- weight_grad: float32 [128, 256], replicated
Inputs may be any that keep to these rules, and one draw needn't show every extreme that they name: Slots at or beyond a cell's tile_count are ignored; some cell is full in every draw. Tile coordinates within a cell may repeat, and repeated tiles add.
All inputs are finite; a program needn't handle non-finite values.
Results may differ from a plain program's by a relative error of at most 0.022.
Values may be sent and summed in bfloat16 or wider, within the bound.
No kernel may reach another device: no remote copies, remote signals or barrier semaphores. Data moves between devices by JAX's collectives and lax.ppermute only.
A program may use at most 64 MiB of HBM per device.

v0:
```python
import jax
import jax.numpy as jnp
from jax import lax
from jax.sharding import PartitionSpec as P


def tile_products(
    tile_block, target_ids, source_ids, tile_total, source, out_blocks, transpose, block_width
):
    source_blocks = source[source_ids]
    if transpose:
        products = jnp.einsum(
            "tij,tif->tjf", tile_block, source_blocks, preferred_element_type=jnp.float32
        )
    else:
        products = jnp.einsum(
            "tij,tjf->tif", tile_block, source_blocks, preferred_element_type=jnp.float32
        )
    slot_ids = jnp.arange(block_width, dtype=jnp.int32)
    live_mask = slot_ids < tile_total
    one_hot = (
        (target_ids[None, :] == jnp.arange(out_blocks, dtype=jnp.int32)[:, None])
        & live_mask[None, :]
    ).astype(jnp.float32)
    return jnp.einsum("rt,tif->rif", one_hot, products, precision=lax.Precision.HIGH)


def spread_tiles(tile_block, target_ids, source_ids, tile_total, source, out_blocks, transpose):
    capacity = tile_block.shape[0]
    return tile_products(
        tile_block, target_ids, source_ids, tile_total, source, out_blocks, transpose, capacity
    )


def on_device(features, weight, tile_values, tile_rows, tile_cols, tile_count, cotangent):
    rows_dev = features.shape[1]
    width_in = features.shape[2]
    tile_size = tile_values.shape[-1]
    row_devices = lax.axis_size("row")
    col_devices = lax.axis_size("col")
    row_tiles = rows_dev * col_devices // tile_size
    col_tiles = rows_dev * row_devices // tile_size
    node_total = rows_dev * row_devices * col_devices
    tile_block = tile_values[0, 0]
    row_ids = tile_rows[0, 0]
    col_ids = tile_cols[0, 0]
    tile_total = tile_count[0, 0]
    gathered = lax.all_gather(features, "row", axis=1, tiled=True)
    col_source = gathered.reshape(col_tiles, tile_size, width_in)
    partial_value = spread_tiles(
        tile_block, row_ids, col_ids, tile_total, col_source, row_tiles, False
    )
    partial_value = partial_value.reshape(row_tiles * tile_size, width_in)
    aggregated = lax.psum_scatter(partial_value, "col", scatter_dimension=0, tiled=True).astype(
        jnp.bfloat16
    )
    pre = jnp.dot(aggregated, weight, preferred_element_type=jnp.float32)
    sigma = jax.nn.sigmoid(pre)
    output = (pre * sigma).astype(jnp.bfloat16)[None]
    slope = sigma * (1.0 + pre * (1.0 - sigma))
    grad_pre = (cotangent[0].astype(jnp.float32) * slope).astype(jnp.bfloat16)
    local_grad = lax.dot_general(
        aggregated, grad_pre, (((0,), (0,)), ((), ())), preferred_element_type=jnp.float32
    )
    weight_grad = lax.psum(local_grad, ("row", "col")) * node_total ** (-0.5)
    full_pre = lax.all_gather(grad_pre, "col", axis=0, tiled=True)
    row_source = lax.dot_general(
        full_pre, weight, (((1,), (1,)), ((), ())), preferred_element_type=jnp.float32
    ).astype(jnp.bfloat16)
    row_source = row_source.reshape(row_tiles, tile_size, width_in)
    partial_back = spread_tiles(
        tile_block, col_ids, row_ids, tile_total, row_source, col_tiles, True
    )
    partial_back = partial_back.reshape(col_tiles * tile_size, width_in)
    grad_features = lax.psum_scatter(
        partial_back.astype(jnp.bfloat16), "row", scatter_dimension=0, tiled=True
    )[None]
    return (output, grad_features, weight_grad)


def solution(mesh):
    placed = (
        P("col", "row", None),
        P(),
        P("row", "col", None, None, None),
        P("row", "col", None),
        P("row", "col", None),
        P("row", "col"),
        P("row", "col", None),
    )
    return jax.shard_map(
        on_device,
        mesh=mesh,
        in_specs=placed,
        out_specs=(P("row", "col", None), P("col", "row", None), P()),
        check_vma=False,
    )
```

profile of v0, /device:TPU:4, one launch (start us, length us, event | category | flops | bytes accessed | tf_op | source)
XLA Modules:
  0.0 752.0 jit_solution(3322477829426455184)
XLA Ops:
  7.2 0.7 all-gather.3.cloned.1.call-update
  8.6 0.7 fusion.27
  9.3 158.5 %all-gather.3.cloned.1.call-done = bf16[1,4096,128]{2,1,0:T(8,128)(2,1)} async-done(((bf16[1,128,128]{2,1,0:T(8,128)(2,1)}), bf16[1,4096,128]{2,1,0:T(8,128)(2,1)}) %all-gather.3.cloned.1.call-update) | async-done | bytes 1048592 | tf_op jit(solution)/shard_map/all_gather | solution.py:48
  167.8 2.9 gather_fusion
  170.7 2.1 fusion.9
  172.8 2.1 copy.12
  174.9 2.1 fusion.2
  177.0 1.3 copy.10
  178.3 0.0 all-gather.5.cloned.1.call-start
  178.3 82.4 %reduce-scatter.3.cloned.1.call-done = f32[128,128]{1,0:T(8,128)} async-done(((f32[2048,128]{1,0:T(8,128)}), f32[128,128]{1,0:T(8,128)}) %reduce-scatter.3.cloned.1.call-update) | async-done | bytes 65552 | tf_op jit(solution)/shard_map/reduce_scatter | solution.py:54
  260.7 1.7 fusion.11
  262.4 0.0 all-reduce.2.cloned.1.call-start
  262.5 1.7 fusion.13
  264.3 0.0 reduce-scatter.5.cloned.1.call-start
  264.3 57.5 %all-gather.5.cloned.1.call-done = bf16[2048,256]{1,0:T(8,128)(2,1)} async-done(((bf16[128,256]{1,0:T(8,128)(2,1)}), bf16[2048,256]{1,0:T(8,128)(2,1)}) %all-gather.5.cloned.1.call-update) | async-done | bytes 1048592 | tf_op jit(solution)/shard_map/all_gather | solution.py:66
  321.8 1.7 convolution_convert_fusion
  323.5 0.8 gather_fusion.1
  324.2 1.9 fusion.7
  326.1 2.4 copy.13
  328.5 0.7 fusion.4
  329.2 1.4 copy.11
  330.6 253.5 %all-reduce.2.cloned.1.call-done = f32[128,256]{1,0:T(8,128)} async-done(((f32[128,256]{1,0:T(8,128)}), f32[128,256]{1,0:T(8,128)}) %all-reduce.2.cloned.1.call-update) | async-done | bytes 131088 | tf_op jit(solution)/shard_map/psum | solution.py:65
  584.2 1.6 broadcast_multiply_fusion
  585.7 159.7 %reduce-scatter.5.cloned.1.call-done = bf16[128,128]{1,0:T(8,128)(2,1)} async-done(((bf16[4096,128]{1,0:T(8,128)(2,1)}), bf16[128,128]{1,0:T(8,128)(2,1)}) %reduce-scatter.5.cloned.1.call-update) | async-done | bytes 32784 | tf_op jit(solution)/shard_map/reduce_scatter | solution.py:75
  (20 shorter events, 0.2 us)
Async XLA Ops:
  7.2 163.5 %copy-start = (bf16[1,1,32,128,128]{4,3,2,1,0:T(8,128)(2,1)S(1)}, bf16[1,1,32,128,128]{4,3,2,1,0:T(8,128)(2,1)}, u32[]{:S(2)}) copy-start(bf16[1,1,32,128,128]{4,3,2,1,0:T(8,128)(2,1)} %param.9) | copy-start | bytes 3145732
  7.2 160.6 %all-gather.3.cloned.1.call-start = ((), (), s32[]{:S(2)}) async-start(), calls=%async_computation.2 | async-start | bytes 1081344 | tf_op jit(solution)/shard_map/all_gather | solution.py:48
  7.9 252.8 %reduce-scatter.3.cloned.1.call-start = ((), (), s32[]{:S(2)}) async-start(), calls=%async_computation.3 | async-start | bytes 1114112 | tf_op jit(solution)/shard_map/reduce_scatter | solution.py:54
  172.8 2.1 copy-start.2
  176.9 83.8 %copy-start.1 = (bf16[128,256]{1,0:T(8,128)(2,1)S(1)}, bf16[128,256]{1,0:T(8,128)(2,1)}, u32[]{:S(2)}) copy-start(bf16[128,256]{1,0:T(8,128)(2,1)} %param.8) | copy-start | bytes 196612
  177.0 83.8 %copy-start.4 = (bf16[1,128,256]{2,1,0:T(8,128)(2,1)S(1)}, bf16[1,128,256]{2,1,0:T(8,128)(2,1)}, u32[]{:S(2)}) copy-start(bf16[1,128,256]{2,1,0:T(8,128)(2,1)} %param.13) | copy-start | bytes 196612
  178.3 143.5 %all-gather.5.cloned.1.call-start = ((), (), s32[]{:S(2)}) async-start(), calls=%async_computation.4 | async-start | bytes 1114112 | tf_op jit(solution)/shard_map/all_gather | solution.py:66
  262.4 321.7 %all-reduce.2.cloned.1.call-start = ((), (), s32[]{:S(2)}) async-start(), calls=%async_computation.6 | async-start | bytes 262144 | tf_op jit(solution)/shard_map/psum | solution.py:65
  264.3 481.2 %reduce-scatter.5.cloned.1.call-start = ((), (), s32[]{:S(2)}) async-start(), calls=%async_computation.5 | async-start | bytes 1081344 | tf_op jit(solution)/shard_map/reduce_scatter | solution.py:75
  326.1 2.4 copy-start.3
Sparse Core Ops, SparseCore 0:
  10.1 157.6 all-gather.2
  178.4 82.2 reduce-scatter.2
  264.5 57.2 all-gather.4
  328.0 256.1 all-reduce.1
  587.4 158.0 reduce-scatter.4
where the time goes:
time: 752 us
  waiting for transfers between devices  712 us (95%)
  between operations  14.5 us (2%)
  matrix products  11.8 us (2%)
  local copies, waits for them, and re-layouts  10.8 us (1%)
    psum x1, waiting for transfers between devices, on_device(): weight_grad = lax.psum(local_grad, ('row', 'col')) * node_total ** (-0.5)  254 us
    reduce_scatter x1, waiting for transfers between devices, on_device(): lax.psum_scatter(partial_back.astype(jnp.bfloat16), 'row', scatter_dimens...  160 us
    all_gather x1, waiting for transfers between devices, on_device(): gathered = lax.all_gather(features, 'row', axis=1, tiled=True)  159 us
    reduce_scatter x1, waiting for transfers between devices, on_device(): lax.psum_scatter(partial_value, 'col', scatter_dimension=0, tiled=True)  82.4 us
    all_gather x1, waiting for transfers between devices, on_device(): full_pre = lax.all_gather(grad_pre, 'col', axis=0, tiled=True)  57.5 us
  transfers between devices with their start and end apart: 5, of which 5 were waited for; matrix products, arithmetic and copies ran while one was open for 2% of the time, Pallas kernels for 0%

commit v1 on v0

--- a/solution.py
+++ b/solution.py
@@ -45,7 +45,9 @@
     row_ids = tile_rows[0, 0]
     col_ids = tile_cols[0, 0]
     tile_total = tile_count[0, 0]
-    gathered = lax.all_gather(features, "row", axis=1, tiled=True)
+    gathered = jnp.concatenate(
+        lax.all_to_all(jnp.stack([features] * lax.axis_size("row")), "row", 0, 0), axis=1
+    )
     col_source = gathered.reshape(col_tiles, tile_size, width_in)
     partial_value = spread_tiles(
         tile_block, row_ids, col_ids, tile_total, col_source, row_tiles, False

time: 752 us -> 638 us (0.85)
  waiting for transfers between devices: 712 us -> 585 us
  starting transfers between devices: 0.2 us -> 13.1 us
    all_gather x1 -> x0, waiting for transfers between devices: 159 us -> none  [on_device(): gathered = lax.all_gather(features, 'row', axis=1, tiled=True)]
    all_to_all x0 -> x1, waiting for transfers between devices: none -> 28.5 us  [on_device(): lax.all_to_all(jnp.stack([features] * lax.axis_size('row')), 'row', 0, 0)]
    all_to_all x0 -> x1, starting transfers between devices: none -> 12.9 us  [on_device(): lax.all_to_all(jnp.stack([features] * lax.axis_size('row')), 'row', 0, 0)]
where the time goes in v1:
time: 638 us
  waiting for transfers between devices  585 us (92%)
  between operations  14.5 us (2%)
  starting transfers between devices  13.1 us (2%)
  matrix products  11.8 us (2%)
  local copies, waits for them, and re-layouts  11.6 us (2%)
    psum x1, waiting for transfers between devices, on_device(): weight_grad = lax.psum(local_grad, ('row', 'col')) * node_total ** (-0.5)  254 us
    reduce_scatter x1, waiting for transfers between devices, on_device(): lax.psum_scatter(partial_back.astype(jnp.bfloat16), 'row', scatter_dimens...  160 us
    reduce_scatter x1, waiting for transfers between devices, on_device(): lax.psum_scatter(partial_value, 'col', scatter_dimension=0, tiled=True)  85.5 us
    all_gather x1, waiting for transfers between devices, on_device(): full_pre = lax.all_gather(grad_pre, 'col', axis=0, tiled=True)  57.4 us
    all_to_all x1, waiting for transfers between devices, on_device(): lax.all_to_all(jnp.stack([features] * lax.axis_size('row')), 'row', 0, 0)  28.5 us
    all_to_all x1, starting transfers between devices, on_device(): lax.all_to_all(jnp.stack([features] * lax.axis_size('row')), 'row', 0, 0)  12.9 us
  transfers between devices with their start and end apart: 5, of which 5 were waited for; matrix products, arithmetic and copies ran while one was open for 2% of the time, Pallas kernels for 0%

profile of v1, /device:TPU:4, one launch (start us, length us, event | category | flops | bytes accessed | tf_op | source)
XLA Modules:
  0.0 637.5 jit_solution(16400471065144516666)
XLA Ops:
  7.2 2.1 stack.2
  9.2 12.9 %all-to-all-start = ((bf16[32,1,128,128]{3,2,1,0:T(8,128)(2,1)}), bf16[32,1,128,128]{3,2,1,0:T(8,128)(2,1)S(1)}, u32[]{:S(2)}, u32[]{:S(2)}) async-start(bf16[32,1,128,128]{3,2,1,0:T(8,128)(2,1)} %stack.2), calls=%async_computation | async-start | bytes 2097152 | tf_op jit(solution)/shard_map/all_to_all | solution.py:49
  22.9 28.5 %all-to-all-done = bf16[32,1,128,128]{3,2,1,0:T(8,128)(2,1)S(1)} async-done(((bf16[32,1,128,128]{3,2,1,0:T(8,128)(2,1)}), bf16[32,1,128,128]{3,2,1,0:T(8,128)(2,1)S(1)}, u32[]{:S(2)}, u32[]{:S(2)}) %all-to-all-start) | async-done | bytes 1048608 | tf_op jit(solution)/shard_map/all_to_all | solution.py:49
  51.4 1.6 gather_fusion
  53.0 2.1 fusion.9
  55.2 2.1 copy.12
  57.2 2.1 fusion.2
  59.3 1.3 copy.10
  60.6 0.0 all-gather.2.cloned.1.call-start
  60.7 85.5 %reduce-scatter.3.cloned.1.call-done = f32[128,128]{1,0:T(8,128)} async-done(((f32[2048,128]{1,0:T(8,128)}), f32[128,128]{1,0:T(8,128)}) %reduce-scatter.3.cloned.1.call-update) | async-done | bytes 65552 | tf_op jit(solution)/shard_map/reduce_scatter | solution.py:56
  146.2 1.7 fusion.11
  147.9 0.0 all-reduce.2.cloned.1.call-start
  148.0 1.7 fusion.13
  149.8 0.0 reduce-scatter.5.cloned.1.call-start
  149.8 57.4 %all-gather.2.cloned.1.call-done = bf16[2048,256]{1,0:T(8,128)(2,1)} async-done(((bf16[128,256]{1,0:T(8,128)(2,1)}), bf16[2048,256]{1,0:T(8,128)(2,1)}) %all-gather.2.cloned.1.call-update) | async-done | bytes 1048592 | tf_op jit(solution)/shard_map/all_gather | solution.py:68
  207.2 1.7 convolution_convert_fusion
  208.9 0.8 gather_fusion.1
  209.6 1.9 fusion.7
  211.5 2.4 copy.13
  213.9 0.7 fusion.4
  214.6 1.4 copy.11
  216.0 253.7 %all-reduce.2.cloned.1.call-done = f32[128,256]{1,0:T(8,128)} async-done(((f32[128,256]{1,0:T(8,128)}), f32[128,256]{1,0:T(8,128)}) %all-reduce.2.cloned.1.call-update) | async-done | bytes 131088 | tf_op jit(solution)/shard_map/psum | solution.py:67
  469.7 1.6 broadcast_multiply_fusion
  471.3 159.7 %reduce-scatter.5.cloned.1.call-done = bf16[128,128]{1,0:T(8,128)(2,1)} async-done(((bf16[4096,128]{1,0:T(8,128)(2,1)}), bf16[128,128]{1,0:T(8,128)(2,1)}) %reduce-scatter.5.cloned.1.call-update) | async-done | bytes 32784 | tf_op jit(solution)/shard_map/reduce_scatter | solution.py:77
  (20 shorter events, 0.2 us)
Async XLA Ops:
  7.2 45.9 %copy-start = (bf16[1,1,32,128,128]{4,3,2,1,0:T(8,128)(2,1)S(1)}, bf16[1,1,32,128,128]{4,3,2,1,0:T(8,128)(2,1)}, u32[]{:S(2)}) copy-start(bf16[1,1,32,128,128]{4,3,2,1,0:T(8,128)(2,1)} %param.9) | copy-start | bytes 3145732
  7.2 15.7 %copy-start.3 = (s32[1,1,32]{2,1,0:T(1,128)S(1)}, s32[1,1,32]{2,1,0:T(1,128)}, u32[]{:S(2)}) copy-start(s32[1,1,32]{2,1,0:T(1,128)} %param.11) | copy-start | bytes 388
  9.2 42.1 %all-to-all-start = ((bf16[32,1,128,128]{3,2,1,0:T(8,128)(2,1)}), bf16[32,1,128,128]{3,2,1,0:T(8,128)(2,1)S(1)}, u32[]{:S(2)}, u32[]{:S(2)}) async-start(bf16[32,1,128,128]{3,2,1,0:T(8,128)(2,1)} %stack.2), calls=%async_computation | async-start | bytes 2097152 | tf_op jit(solution)/shard_map/all_to_all | solution.py:49
  22.2 124.0 %reduce-scatter.3.cloned.1.call-start = ((), (), s32[]{:S(2)}) async-start(), calls=%async_computation.3 | async-start | bytes 1114112 | tf_op jit(solution)/shard_map/reduce_scatter | solution.py:56
  55.2 2.1 copy-start.2
  59.3 86.9 %copy-start.1 = (bf16[128,256]{1,0:T(8,128)(2,1)S(1)}, bf16[128,256]{1,0:T(8,128)(2,1)}, u32[]{:S(2)}) copy-start(bf16[128,256]{1,0:T(8,128)(2,1)} %param.8) | copy-start | bytes 196612
  59.3 86.9 %copy-start.4 = (bf16[1,128,256]{2,1,0:T(8,128)(2,1)S(1)}, bf16[1,128,256]{2,1,0:T(8,128)(2,1)}, u32[]{:S(2)}) copy-start(bf16[1,128,256]{2,1,0:T(8,128)(2,1)} %param.13) | copy-start | bytes 196612
  60.6 146.6 %all-gather.2.cloned.1.call-start = ((), (), s32[]{:S(2)}) async-start(), calls=%async_computation.4 | async-start | bytes 1114112 | tf_op jit(solution)/shard_map/all_gather | solution.py:68
  147.9 321.8 %all-reduce.2.cloned.1.call-start = ((), (), s32[]{:S(2)}) async-start(), calls=%async_computation.6 | async-start | bytes 262144 | tf_op jit(solution)/shard_map/psum | solution.py:67
  149.8 481.2 %reduce-scatter.5.cloned.1.call-start = ((), (), s32[]{:S(2)}) async-start(), calls=%async_computation.5 | async-start | bytes 1081344 | tf_op jit(solution)/shard_map/reduce_scatter | solution.py:77
Sparse Core Ops, SparseCore 0:
  60.8 85.4 reduce-scatter.2
  150.0 57.1 all-gather.1
  213.6 256.1 all-reduce.1
  472.9 158.0 reduce-scatter.4
